TPU v7x, 32 devices: a whole 2x2x4 slice. The times are simulated.
32 devices in a mesh: grp: 2 (over x), xy: 4 (over y, core), gz: 4 (over z).
Axes of the slice: x: 2, y: 2, z: 4, core: 2. Of those that a mesh axis runs over, the one named last changes fastest.
Arguments:
- fields: float32 [12, 16, 64, 512], P('grp', 'xy', 'gz'), parts along dimension 0, may hold values from -6 to 6
- adjoint_fields: float32 [12, 16, 64, 512], P('grp', 'xy', 'gz'), parts along dimension 0, may hold values from -6 to 6
- material_ids: int32 [16, 64, 1024], P('xy', 'gz', 'grp'), parts along dimension 2, may hold values from 0 to 3
- material_eps: float32 [4], replicated, may hold values from 1 to 12
- monitor_cells: int32 [4, 4, 2048], P('xy', 'gz', 'grp'), parts along dimension 2, may hold values from 0 to 32767
- monitor_bins: int32 [4, 4, 2048], P('xy', 'gz', 'grp'), parts along dimension 2, may hold values from 0 to 127
- source_cells: int32 [4, 4, 2048], P('xy', 'gz', 'grp'), parts along dimension 2, may hold values from 0 to 32767
- source_bins: int32 [4, 4, 2048], P('xy', 'gz', 'grp'), parts along dimension 2, may hold values from 0 to 127
- bin_weight: float32 [256], P('grp'), parts along dimension 0, may hold values from 0.5 to 2
Outputs:
- forward_out: float32 [12, 16, 64, 512], P('grp', 'xy', 'gz'), parts along dimension 0
- adjoint_out: float32 [12, 16, 64, 512], P('grp', 'xy', 'gz'), parts along dimension 0
- monitor_dft: float32 [16, 128], P('grp', ('xy', 'gz')), parts along dimension 0
There are 2 independent parts, one for each index of `grp`. A program takes and returns all parts, laid end to end along the dimension named above; an argument that names none is the same for every part. Nothing has to cross between parts.
All inputs are finite; a program needn't handle non-finite values.
Results may differ from a plain program's by a relative error of at most 0.00011.
Values sent between devices are 32-bit elements; how exact they have to be, the bound alone decides.
No kernel may reach another device: no remote copies, remote signals or barrier semaphores. Data moves between devices by JAX's collectives and lax.ppermute only.
A program may use at most 64 MiB of HBM per device.

v0:
```python
import jax
import jax.numpy as jnp
from jax import lax
from jax.sharding import PartitionSpec as P

STEPS = 8
NFREQ = 4
STEP_RATIO = 0.5


def from_behind(value, axis, steps):
    count = lax.axis_size(axis)
    first, last = (max(0, -steps), min(count, count - steps))
    return lax.ppermute(value, axis, [(source, source + steps) for source in range(first, last)])


def forward_diff(values, after, along):
    upper = jnp.concatenate(
        [
            lax.slice_in_dim(values, 1, values.shape[along], axis=along),
            jnp.expand_dims(after, along),
        ],
        axis=along,
    )
    return upper - values


def backward_diff(values, before, along):
    lower = jnp.concatenate(
        [
            jnp.expand_dims(before, along),
            lax.slice_in_dim(values, 0, values.shape[along] - 1, axis=along),
        ],
        axis=along,
    )
    return values - lower


def across_x(plane, offset):
    return from_behind(plane, "xy", offset)


def across_z(plane, offset):
    return from_behind(plane, "gz", offset)


def update_magnetic(electric, magnetic):
    electric_x, electric_y, electric_z = electric
    magnetic_x, magnetic_y, magnetic_z = magnetic
    x_next = across_x(jnp.stack([electric_y[0], electric_z[0]]), -1)
    z_next = across_z(jnp.stack([electric_x[:, 0], electric_y[:, 0]]), -1)
    zero_y = jnp.zeros_like(electric_x[:, :, 0])
    magnetic_x = magnetic_x - STEP_RATIO * (
        forward_diff(electric_z, zero_y, 2) - forward_diff(electric_y, z_next[1], 1)
    )
    magnetic_y = magnetic_y - STEP_RATIO * (
        forward_diff(electric_x, z_next[0], 1) - forward_diff(electric_z, x_next[1], 0)
    )
    magnetic_z = magnetic_z - STEP_RATIO * (
        forward_diff(electric_y, x_next[0], 0) - forward_diff(electric_x, zero_y, 2)
    )
    return (magnetic_x, magnetic_y, magnetic_z)


def update_electric(electric, magnetic, inverse):
    electric_x, electric_y, electric_z = electric
    magnetic_x, magnetic_y, magnetic_z = magnetic
    x_prev = across_x(jnp.stack([magnetic_y[-1], magnetic_z[-1]]), 1)
    z_prev = across_z(jnp.stack([magnetic_x[:, -1], magnetic_y[:, -1]]), 1)
    zero_y = jnp.zeros_like(electric_x[:, :, 0])
    electric_x = electric_x + STEP_RATIO * inverse * (
        backward_diff(magnetic_z, zero_y, 2) - backward_diff(magnetic_y, z_prev[1], 1)
    )
    electric_y = electric_y + STEP_RATIO * inverse * (
        backward_diff(magnetic_x, z_prev[0], 1) - backward_diff(magnetic_z, x_prev[1], 0)
    )
    electric_z = electric_z + STEP_RATIO * inverse * (
        backward_diff(magnetic_y, x_prev[0], 0) - backward_diff(magnetic_x, zero_y, 2)
    )
    return (electric_x, electric_y, electric_z)


def inverse_permittivity(material_ids, material_eps):
    result = jnp.zeros(material_ids.shape, jnp.float32)
    for material in range(material_eps.shape[0]):
        result = jnp.where(material_ids == material, 1.0 / material_eps[material], result)
    return result


def time_kernels(count):
    times = jnp.arange(count, dtype=jnp.float32) + 1.0
    omegas = 0.3 + 0.35 * jnp.arange(NFREQ, dtype=jnp.float32)
    phases = times[:, None] * omegas[None, :]
    record_kernel = jnp.concatenate([jnp.cos(phases), -jnp.sin(phases)], axis=1)
    reverse = count - jnp.arange(count, dtype=jnp.float32)
    back_phases = reverse[:, None] * omegas[None, :]
    source_kernel = jnp.concatenate([jnp.cos(back_phases), jnp.sin(back_phases)], axis=1)
    return (record_kernel, source_kernel)


def normalize(totals, weights):
    real_part = totals[:NFREQ]
    imag_part = totals[NFREQ:]
    scale = weights[None, :] / jnp.sqrt(1.0 + real_part * real_part + imag_part * imag_part)
    return jnp.concatenate([real_part * scale, imag_part * scale], axis=0)


def local(
    fields,
    adjoint_fields,
    material_ids,
    material_eps,
    monitor_cells,
    monitor_bins,
    source_cells,
    source_bins,
    bin_weight,
):
    inverse = inverse_permittivity(material_ids, material_eps)
    record_kernel, source_kernel = time_kernels(STEPS)
    watched = monitor_cells.reshape(-1)
    electric = (fields[0], fields[1], fields[2])
    magnetic = (fields[3], fields[4], fields[5])
    records = []
    for step_index in range(STEPS):
        magnetic = update_magnetic(electric, magnetic)
        electric = update_electric(electric, magnetic, inverse)
        records.append(electric[2].reshape(-1)[watched])
    forward_out = jnp.stack(list(electric) + list(magnetic))
    samples = jnp.stack(records)
    partial_dft = jnp.dot(samples.T, record_kernel, precision=lax.Precision.HIGHEST)
    bin_table = jax.ops.segment_sum(
        partial_dft, monitor_bins.reshape(-1), num_segments=bin_weight.shape[0]
    ).T
    owners = lax.axis_size("xy") * lax.axis_size("gz")
    own_count = bin_table.shape[1] // owners
    device_rank = lax.axis_index(("xy", "gz"))
    monitor_dft = lax.psum_scatter(bin_table, ("xy", "gz"), scatter_dimension=1, tiled=True)
    own_weight = lax.dynamic_slice_in_dim(bin_weight, device_rank * own_count, own_count)
    coefficients = lax.all_gather(
        normalize(monitor_dft, own_weight), ("xy", "gz"), axis=1, tiled=True
    )
    picked = jnp.take(coefficients, source_bins.reshape(-1), axis=1)
    amplitudes = jnp.dot(source_kernel, picked, precision=lax.Precision.HIGHEST)
    targets = source_cells.reshape(-1)
    electric = (adjoint_fields[0], adjoint_fields[1], adjoint_fields[2])
    magnetic = (adjoint_fields[3], adjoint_fields[4], adjoint_fields[5])
    for step_index in range(STEPS):
        magnetic = update_magnetic(electric, magnetic)
        electric = update_electric(electric, magnetic, inverse)
        driven = (
            electric[2]
            .reshape(-1)
            .at[targets]
            .add(amplitudes[step_index])
            .reshape(electric[2].shape)
        )
        electric = (electric[0], electric[1], driven)
    adjoint_out = jnp.stack(list(electric) + list(magnetic))
    return (forward_out, adjoint_out, monitor_dft)


def solution(mesh):
    placed = (
        P("grp", "xy", "gz", None),
        P("grp", "xy", "gz", None),
        P("xy", "gz", "grp"),
        P(),
        P("xy", "gz", "grp"),
        P("xy", "gz", "grp"),
        P("xy", "gz", "grp"),
        P("xy", "gz", "grp"),
        P("grp"),
    )
    return jax.shard_map(
        local,
        mesh=mesh,
        in_specs=placed,
        out_specs=(P("grp", "xy", "gz", None), P("grp", "xy", "gz", None), P("grp", ("xy", "gz"))),
        check_vma=False,
    )
```

profile of v0, /device:TPU:1, one launch (start us, length us, event | category | flops | bytes accessed | tf_op | source)
XLA Modules:
  0.0 464.7 jit_solution(17606218398477818462)
XLA Ops:
  25.1 5.9 %collective-permute-start.34 = (f32[2,4,512]{2,0,1:T(2,128)S(1)}, f32[2,4,512]{2,0,1:T(2,128)S(1)}, u32[]{:S(2)}, u32[]{:S(2)}) collective-permute-start(f32[2,4,512]{2,0,1:T(2,128)S(1)} %pad_maximum_fusion.49), channel_id=1, source_target_pairs={{0,1},{1,2},{2,3},{4,5},{5,6},{6,7},{8,9},{9,10},{10,11},{12,13},{... | collective-permute-start | bytes 49160 | tf_op jit(solution)/shard_map/ppermute | solution.py:14
  48.9 10.5 %gather_fusion = f32[1024]{0:T(1024)} fusion(f32[32768]{0:T(1024)S(1)} %bitcast.501, s32[1024]{0:T(1024)S(1)} %broadcast_clamp_fusion.1), kind=kCustom, calls=%fused_computation | custom fusion | bytes 12288 | tf_op jit(solution)/shard_map/gather | solution.py:128
  77.9 6.2 %gather_fusion.1 = f32[1024]{0:T(1024)S(1)} fusion(f32[32768]{0:T(1024)S(1)} %bitcast.502, s32[1024]{0:T(1024)S(1)} %broadcast_clamp_fusion.1), kind=kCustom, calls=%fused_computation.1 | custom fusion | bytes 12288 | tf_op jit(solution)/shard_map/gather | solution.py:128
  97.2 6.2 %gather_fusion.2 = f32[1024]{0:T(1024)S(1)} fusion(f32[32768]{0:T(1024)S(1)} %bitcast.503, s32[1024]{0:T(1024)S(1)} %broadcast_clamp_fusion.1), kind=kCustom, calls=%fused_computation.2 | custom fusion | bytes 12288 | tf_op jit(solution)/shard_map/gather | solution.py:128
  107.7 4.8 %collective-permute-start.15 = (f32[2,16,512]{2,1,0:T(8,128)S(1)}, f32[2,16,512]{2,1,0:T(8,128)S(1)}, u32[]{:S(2)}, u32[]{:S(2)}) collective-permute-start(f32[2,16,512]{2,1,0:T(8,128)S(1)} %pad_maximum_fusion.7), channel_id=1, source_target_pairs={{0,4},{4,8},{8,12},{1,5},{5,9},{9,13},{2,6},{6,10},{10,14},{3,7},{... | collective-permute-start | bytes 196616 | tf_op jit(solution)/shard_map/ppermute | solution.py:14
  117.5 6.2 %gather_fusion.3 = f32[1024]{0:T(1024)S(1)} fusion(f32[32768]{0:T(1024)S(1)} %bitcast.504, s32[1024]{0:T(1024)S(1)} %broadcast_clamp_fusion.1), kind=kCustom, calls=%fused_computation.3 | custom fusion | bytes 12288 | tf_op jit(solution)/shard_map/gather | solution.py:128
  128.1 4.8 %collective-permute-start.19 = (f32[2,16,512]{2,1,0:T(8,128)S(1)}, f32[2,16,512]{2,1,0:T(8,128)S(1)}, u32[]{:S(2)}, u32[]{:S(2)}) collective-permute-start(f32[2,16,512]{2,1,0:T(8,128)S(1)} %pad_maximum_fusion.9), channel_id=1, source_target_pairs={{0,4},{4,8},{8,12},{1,5},{5,9},{9,13},{2,6},{6,10},{10,14},{3,7},{... | collective-permute-start | bytes 196616 | tf_op jit(solution)/shard_map/ppermute | solution.py:14
  137.9 6.2 %gather_fusion.4 = f32[1024]{0:T(1024)S(1)} fusion(f32[32768]{0:T(1024)S(1)} %bitcast.505, s32[1024]{0:T(1024)S(1)} %broadcast_clamp_fusion.1), kind=kCustom, calls=%fused_computation.4 | custom fusion | bytes 12288 | tf_op jit(solution)/shard_map/gather | solution.py:128
  148.4 4.8 %collective-permute-start.23 = (f32[2,16,512]{2,1,0:T(8,128)S(1)}, f32[2,16,512]{2,1,0:T(8,128)S(1)}, u32[]{:S(2)}, u32[]{:S(2)}) collective-permute-start(f32[2,16,512]{2,1,0:T(8,128)S(1)} %pad_maximum_fusion.11), channel_id=1, source_target_pairs={{0,4},{4,8},{8,12},{1,5},{5,9},{9,13},{2,6},{6,10},{10,14},{3,7},{... | collective-permute-start | bytes 196616 | tf_op jit(solution)/shard_map/ppermute | solution.py:14
  158.2 6.2 %gather_fusion.5 = f32[1024]{0:T(1024)S(1)} fusion(f32[32768]{0:T(1024)S(1)} %bitcast.506, s32[1024]{0:T(1024)S(1)} %broadcast_clamp_fusion.1), kind=kCustom, calls=%fused_computation.5 | custom fusion | bytes 12288 | tf_op jit(solution)/shard_map/gather | solution.py:128
  178.7 6.2 %gather_fusion.6 = f32[1024]{0:T(1024)S(1)} fusion(f32[32768]{0:T(1024)S(1)} %bitcast.507, s32[1024]{0:T(1024)S(1)} %broadcast_clamp_fusion.1), kind=kCustom, calls=%fused_computation.6 | custom fusion | bytes 12288 | tf_op jit(solution)/shard_map/gather | solution.py:128
  195.7 6.2 %gather_fusion.7 = f32[1024]{0:T(1024)S(1)} fusion(f32[32768]{0:T(1024)S(1)} %bitcast.500, s32[1024]{0:T(1024)S(1)} %broadcast_clamp_fusion.1), kind=kCustom, calls=%fused_computation.7 | custom fusion | bytes 12288 | tf_op jit(solution)/shard_map/gather | solution.py:128
  204.2 6.2 %scatter_custom_fusion = f32[128,8]{1,0:T(8,128)S(1)} fusion(s32[1024]{0:T(1024)} %bitcast.616, f32[1024,8]{1,0:T(8,128)S(1)} %fusion.306, f32[]{:T(128)} %constant.24.clone.1), kind=kCustom, calls=%fused_computation.496 | custom fusion | flops 8192 | bytes 4608 | tf_op jit(solution)/shard_map/scatter-add | solution.py:132
  210.4 55.7 %all-reduce.64 = f32[8,128]{0,1:T(8,128)S(1)} all-reduce(f32[8,128]{0,1:T(8,128)S(1)} %bitcast.596), channel_id=2, replica_groups=mesh['grp'=2,'xy'=4,'gz'=4] {'xy','gz'}, use_global_device_ids=true, to_apply=%region_1.2.clone | all-reduce | flops 1024 | bytes 8192
  267.0 29.0 %all_gather.3 = f32[8,128]{0,1:T(8,128)S(1)} all-gather(f32[8,8]{0,1:T(8,128)S(1)} %pad_maximum_fusion.64), channel_id=1, replica_groups=mesh['grp'=2,'xy'=4,'gz'=4] {'xy','gz'}, dimensions={1}, use_global_device_ids=true | all-gather | bytes 4352 | tf_op jit(solution)/shard_map/all_gather | solution.py:140
  300.1 6.1 %scatter_fusion = f32[32768]{0:T(1024)S(1)} fusion(f32[32768]{0:T(1024)S(1)} %bitcast.492, s32[1024]{0:T(1024)S(1)} %bitcast.588, f32[1024]{0:T(1024)S(1)} %bitcast.604), kind=kCustom, calls=%fused_computation.10 | custom fusion | flops 1024 | bytes 16384 | tf_op jit(solution)/shard_map/scatter-add | solution.py:155
  307.0 5.4 %collective-permute-start.36 = (f32[2,16,512]{2,1,0:T(8,128)S(1)}, f32[2,16,512]{2,1,0:T(8,128)S(1)}, u32[]{:S(2)}, u32[]{:S(2)}) collective-permute-start(f32[2,16,512]{2,1,0:T(8,128)S(1)} %pad_maximum_fusion.18), channel_id=1, source_target_pairs={{4,0},{8,4},{12,8},{5,1},{9,5},{13,9},{6,2},{10,6},{14,10},{7,3},{... | collective-permute-start | bytes 196616 | tf_op jit(solution)/shard_map/ppermute | solution.py:14
  325.0 6.1 %scatter_fusion.1 = f32[32768]{0:T(1024)S(1)} fusion(f32[32768]{0:T(1024)S(1)} %bitcast.493, s32[1024]{0:T(1024)S(1)} %bitcast.589, f32[1024]{0:T(1024)S(1)} %bitcast.603), kind=kCustom, calls=%fused_computation.11 | custom fusion | flops 1024 | bytes 16384 | tf_op jit(solution)/shard_map/scatter-add | solution.py:155
  347.1 6.1 %scatter_fusion.2 = f32[32768]{0:T(1024)S(1)} fusion(f32[32768]{0:T(1024)S(1)} %bitcast.494, s32[1024]{0:T(1024)S(1)} %bitcast.590, f32[1024]{0:T(1024)S(1)} %bitcast.602), kind=kCustom, calls=%fused_computation.12 | custom fusion | flops 1024 | bytes 16384 | tf_op jit(solution)/shard_map/scatter-add | solution.py:155
  369.2 6.1 %scatter_fusion.3 = f32[32768]{0:T(1024)S(1)} fusion(f32[32768]{0:T(1024)S(1)} %bitcast.495, s32[1024]{0:T(1024)S(1)} %bitcast.591, f32[1024]{0:T(1024)S(1)} %bitcast.601), kind=kCustom, calls=%fused_computation.13 | custom fusion | flops 1024 | bytes 16384 | tf_op jit(solution)/shard_map/scatter-add | solution.py:155
  391.3 6.1 %scatter_fusion.4 = f32[32768]{0:T(1024)S(1)} fusion(f32[32768]{0:T(1024)S(1)} %bitcast.496, s32[1024]{0:T(1024)S(1)} %bitcast.592, f32[1024]{0:T(1024)S(1)} %bitcast.600), kind=kCustom, calls=%fused_computation.14 | custom fusion | flops 1024 | bytes 16384 | tf_op jit(solution)/shard_map/scatter-add | solution.py:155
  413.4 6.1 %scatter_fusion.5 = f32[32768]{0:T(1024)S(1)} fusion(f32[32768]{0:T(1024)S(1)} %bitcast.497, s32[1024]{0:T(1024)S(1)} %bitcast.593, f32[1024]{0:T(1024)S(1)} %bitcast.599), kind=kCustom, calls=%fused_computation.15 | custom fusion | flops 1024 | bytes 16384 | tf_op jit(solution)/shard_map/scatter-add | solution.py:155
  435.4 6.1 %scatter_fusion.6 = f32[32768]{0:T(1024)S(1)} fusion(f32[32768]{0:T(1024)S(1)} %bitcast.498, s32[1024]{0:T(1024)S(1)} %bitcast.594, f32[1024]{0:T(1024)S(1)} %bitcast.598), kind=kCustom, calls=%fused_computation.16 | custom fusion | flops 1024 | bytes 16384 | tf_op jit(solution)/shard_map/scatter-add | solution.py:155
  457.5 6.1 %scatter_fusion.7 = f32[32768]{0:T(1024)S(1)} fusion(f32[32768]{0:T(1024)S(1)} %bitcast.499, s32[1024]{0:T(1024)S(1)} %bitcast.595, f32[1024]{0:T(1024)S(1)} %bitcast.597), kind=kCustom, calls=%fused_computation.17 | custom fusion | flops 1024 | bytes 16384 | tf_op jit(solution)/shard_map/scatter-add | solution.py:155
  (666 shorter events, 236.8 us)
Async XLA Ops:
  2.1 21.9 %collective-permute-start.32 = (f32[2,16,512]{2,1,0:T(8,128)}, f32[2,16,512]{2,1,0:T(8,128)}, u32[]{:S(2)}, u32[]{:S(2)}) collective-permute-start(f32[2,16,512]{2,1,0:T(8,128)} %pad_maximum_fusion.16), channel_id=1, source_target_pairs={{4,0},{8,4},{12,8},{5,1},{9,5},{13,9},{6,2},{10,6},{14,10},{7,3},{... | collective-permute-start | bytes 196616 | tf_op jit(solution)/shard_map/ppermute | solution.py:14
  5.8 16.3 %collective-permute-start.33 = (f32[2,4,512]{2,0,1:T(2,128)}, f32[2,4,512]{2,0,1:T(2,128)}, u32[]{:S(2)}, u32[]{:S(2)}) collective-permute-start(f32[2,4,512]{2,0,1:T(2,128)} %pad_maximum_fusion.48), channel_id=1, source_target_pairs={{1,0},{2,1},{3,2},{5,4},{6,5},{7,6},{9,8},{10,9},{11,10},{13,12},{... | collective-permute-start | bytes 49160 | tf_op jit(solution)/shard_map/ppermute | solution.py:14
  7.1 16.6 %collective-permute-start = (f32[2,16,512]{2,1,0:T(8,128)S(1)}, f32[2,16,512]{2,1,0:T(8,128)S(1)}, u32[]{:S(2)}, u32[]{:S(2)}) collective-permute-start(f32[2,16,512]{2,1,0:T(8,128)S(1)} %pad_maximum_fusion), channel_id=1, source_target_pairs={{4,0},{8,4},{12,8},{5,1},{9,5},{13,9},{6,2},{10,6},{14,10},{7,3},{... | collective-permute-start | bytes 196616 | tf_op jit(solution)/shard_map/ppermute | solution.py:14
  9.7 13.2 %collective-permute-start.1 = (f32[2,4,512]{2,0,1:T(2,128)}, f32[2,4,512]{2,0,1:T(2,128)}, u32[]{:S(2)}, u32[]{:S(2)}) collective-permute-start(f32[2,4,512]{2,0,1:T(2,128)} %pad_maximum_fusion.32), channel_id=1, source_target_pairs={{1,0},{2,1},{3,2},{5,4},{6,5},{7,6},{9,8},{10,9},{11,10},{13,12},{... | collective-permute-start | bytes 49160 | tf_op jit(solution)/shard_map/ppermute | solution.py:14
  25.1 16.1 %collective-permute-start.34 = (f32[2,4,512]{2,0,1:T(2,128)S(1)}, f32[2,4,512]{2,0,1:T(2,128)S(1)}, u32[]{:S(2)}, u32[]{:S(2)}) collective-permute-start(f32[2,4,512]{2,0,1:T(2,128)S(1)} %pad_maximum_fusion.49), channel_id=1, source_target_pairs={{0,1},{1,2},{2,3},{4,5},{5,6},{6,7},{8,9},{9,10},{10,11},{12,13},{... | collective-permute-start | bytes 49160 | tf_op jit(solution)/shard_map/ppermute | solution.py:14
  31.1 10.0 %collective-permute-start.2 = (f32[2,4,512]{2,0,1:T(2,128)S(1)}, f32[2,4,512]{2,0,1:T(2,128)S(1)}, u32[]{:S(2)}, u32[]{:S(2)}) collective-permute-start(f32[2,4,512]{2,0,1:T(2,128)S(1)} %pad_maximum_fusion.33), channel_id=1, source_target_pairs={{0,1},{1,2},{2,3},{4,5},{5,6},{6,7},{8,9},{9,10},{10,11},{12,13},{... | collective-permute-start | bytes 49160 | tf_op jit(solution)/shard_map/ppermute | solution.py:14
  42.9 16.6 %collective-permute-start.5 = (f32[2,4,512]{2,0,1:T(2,128)S(1)}, f32[2,4,512]{2,0,1:T(2,128)S(1)}, u32[]{:S(2)}, u32[]{:S(2)}) collective-permute-start(f32[2,4,512]{2,0,1:T(2,128)S(1)} %pad_maximum_fusion.34), channel_id=1, source_target_pairs={{1,0},{2,1},{3,2},{5,4},{6,5},{7,6},{9,8},{10,9},{11,10},{13,12},{... | collective-permute-start | bytes 49160 | tf_op jit(solution)/shard_map/ppermute | solution.py:14
  46.4 13.1 %collective-permute-start.4 = (f32[2,16,512]{2,1,0:T(8,128)S(1)}, f32[2,16,512]{2,1,0:T(8,128)S(1)}, u32[]{:S(2)}, u32[]{:S(2)}) collective-permute-start(f32[2,16,512]{2,1,0:T(8,128)S(1)} %pad_maximum_fusion.2), channel_id=1, source_target_pairs={{4,0},{8,4},{12,8},{5,1},{9,5},{13,9},{6,2},{10,6},{14,10},{7,3},{... | collective-permute-start | bytes 196616 | tf_op jit(solution)/shard_map/ppermute | solution.py:14
  65.2 8.9 %collective-permute-start.7 = (f32[2,16,512]{2,1,0:T(8,128)S(1)}, f32[2,16,512]{2,1,0:T(8,128)S(1)}, u32[]{:S(2)}, u32[]{:S(2)}) collective-permute-start(f32[2,16,512]{2,1,0:T(8,128)S(1)} %pad_maximum_fusion.3), channel_id=1, source_target_pairs={{0,4},{4,8},{8,12},{1,5},{5,9},{9,13},{2,6},{6,10},{10,14},{3,7},{... | collective-permute-start | bytes 196616 | tf_op jit(solution)/shard_map/ppermute | solution.py:14
  74.3 9.7 %collective-permute-start.9 = (f32[2,4,512]{2,0,1:T(2,128)S(1)}, f32[2,4,512]{2,0,1:T(2,128)S(1)}, u32[]{:S(2)}, u32[]{:S(2)}) collective-permute-start(f32[2,4,512]{2,0,1:T(2,128)S(1)} %pad_maximum_fusion.36), channel_id=1, source_target_pairs={{1,0},{2,1},{3,2},{5,4},{6,5},{7,6},{9,8},{10,9},{11,10},{13,12},{... | collective-permute-start | bytes 49160 | tf_op jit(solution)/shard_map/ppermute | solution.py:14
  75.8 8.3 %collective-permute-start.8 = (f32[2,16,512]{2,1,0:T(8,128)S(1)}, f32[2,16,512]{2,1,0:T(8,128)S(1)}, u32[]{:S(2)}, u32[]{:S(2)}) collective-permute-start(f32[2,16,512]{2,1,0:T(8,128)S(1)} %pad_maximum_fusion.4), channel_id=1, source_target_pairs={{4,0},{8,4},{12,8},{5,1},{9,5},{13,9},{6,2},{10,6},{14,10},{7,3},{... | collective-permute-start | bytes 196616 | tf_op jit(solution)/shard_map/ppermute | solution.py:14
  93.8 9.6 %collective-permute-start.13 = (f32[2,4,512]{2,0,1:T(2,128)S(1)}, f32[2,4,512]{2,0,1:T(2,128)S(1)}, u32[]{:S(2)}, u32[]{:S(2)}) collective-permute-start(f32[2,4,512]{2,0,1:T(2,128)S(1)} %pad_maximum_fusion.38), channel_id=1, source_target_pairs={{1,0},{2,1},{3,2},{5,4},{6,5},{7,6},{9,8},{10,9},{11,10},{13,12},{... | collective-permute-start | bytes 49160 | tf_op jit(solution)/shard_map/ppermute | solution.py:14
  95.2 8.2 %collective-permute-start.12 = (f32[2,16,512]{2,1,0:T(8,128)S(1)}, f32[2,16,512]{2,1,0:T(8,128)S(1)}, u32[]{:S(2)}, u32[]{:S(2)}) collective-permute-start(f32[2,16,512]{2,1,0:T(8,128)S(1)} %pad_maximum_fusion.6), channel_id=1, source_target_pairs={{4,0},{8,4},{12,8},{5,1},{9,5},{13,9},{6,2},{10,6},{14,10},{7,3},{... | collective-permute-start | bytes 196616 | tf_op jit(solution)/shard_map/ppermute | solution.py:14
  103.7 8.9 %collective-permute-start.14 = (f32[2,4,512]{2,0,1:T(2,128)S(1)}, f32[2,4,512]{2,0,1:T(2,128)S(1)}, u32[]{:S(2)}, u32[]{:S(2)}) collective-permute-start(f32[2,4,512]{2,0,1:T(2,128)S(1)} %pad_maximum_fusion.39), channel_id=1, source_target_pairs={{0,1},{1,2},{2,3},{4,5},{5,6},{6,7},{8,9},{9,10},{10,11},{12,13},{... | collective-permute-start | bytes 49160 | tf_op jit(solution)/shard_map/ppermute | solution.py:14
  114.1 9.6 %collective-permute-start.17 = (f32[2,4,512]{2,0,1:T(2,128)S(1)}, f32[2,4,512]{2,0,1:T(2,128)S(1)}, u32[]{:S(2)}, u32[]{:S(2)}) collective-permute-start(f32[2,4,512]{2,0,1:T(2,128)S(1)} %pad_maximum_fusion.40), channel_id=1, source_target_pairs={{1,0},{2,1},{3,2},{5,4},{6,5},{7,6},{9,8},{10,9},{11,10},{13,12},{... | collective-permute-start | bytes 49160 | tf_op jit(solution)/shard_map/ppermute | solution.py:14
  124.0 8.9 %collective-permute-start.18 = (f32[2,4,512]{2,0,1:T(2,128)S(1)}, f32[2,4,512]{2,0,1:T(2,128)S(1)}, u32[]{:S(2)}, u32[]{:S(2)}) collective-permute-start(f32[2,4,512]{2,0,1:T(2,128)S(1)} %pad_maximum_fusion.41), channel_id=1, source_target_pairs={{0,1},{1,2},{2,3},{4,5},{5,6},{6,7},{8,9},{9,10},{10,11},{12,13},{... | collective-permute-start | bytes 49160 | tf_op jit(solution)/shard_map/ppermute | solution.py:14
  134.4 9.6 %collective-permute-start.21 = (f32[2,4,512]{2,0,1:T(2,128)S(1)}, f32[2,4,512]{2,0,1:T(2,128)S(1)}, u32[]{:S(2)}, u32[]{:S(2)}) collective-permute-start(f32[2,4,512]{2,0,1:T(2,128)S(1)} %pad_maximum_fusion.42), channel_id=1, source_target_pairs={{1,0},{2,1},{3,2},{5,4},{6,5},{7,6},{9,8},{10,9},{11,10},{13,12},{... | collective-permute-start | bytes 49160 | tf_op jit(solution)/shard_map/ppermute | solution.py:14
  135.9 8.2 %collective-permute-start.20 = (f32[2,16,512]{2,1,0:T(8,128)S(1)}, f32[2,16,512]{2,1,0:T(8,128)S(1)}, u32[]{:S(2)}, u32[]{:S(2)}) collective-permute-start(f32[2,16,512]{2,1,0:T(8,128)S(1)} %pad_maximum_fusion.10), channel_id=1, source_target_pairs={{4,0},{8,4},{12,8},{5,1},{9,5},{13,9},{6,2},{10,6},{14,10},{7,3},{... | collective-permute-start | bytes 196616 | tf_op jit(solution)/shard_map/ppermute | solution.py:14
  144.3 8.9 %collective-permute-start.22 = (f32[2,4,512]{2,0,1:T(2,128)S(1)}, f32[2,4,512]{2,0,1:T(2,128)S(1)}, u32[]{:S(2)}, u32[]{:S(2)}) collective-permute-start(f32[2,4,512]{2,0,1:T(2,128)S(1)} %pad_maximum_fusion.43), channel_id=1, source_target_pairs={{0,1},{1,2},{2,3},{4,5},{5,6},{6,7},{8,9},{9,10},{10,11},{12,13},{... | collective-permute-start | bytes 49160 | tf_op jit(solution)/shard_map/ppermute | solution.py:14
  154.8 9.6 %collective-permute-start.25 = (f32[2,4,512]{2,0,1:T(2,128)S(1)}, f32[2,4,512]{2,0,1:T(2,128)S(1)}, u32[]{:S(2)}, u32[]{:S(2)}) collective-permute-start(f32[2,4,512]{2,0,1:T(2,128)S(1)} %pad_maximum_fusion.44), channel_id=1, source_target_pairs={{1,0},{2,1},{3,2},{5,4},{6,5},{7,6},{9,8},{10,9},{11,10},{13,12},{... | collective-permute-start | bytes 49160 | tf_op jit(solution)/shard_map/ppermute | solution.py:14
  164.7 8.9 %collective-permute-start.26 = (f32[2,4,512]{2,0,1:T(2,128)S(1)}, f32[2,4,512]{2,0,1:T(2,128)S(1)}, u32[]{:S(2)}, u32[]{:S(2)}) collective-permute-start(f32[2,4,512]{2,0,1:T(2,128)S(1)} %pad_maximum_fusion.45), channel_id=1, source_target_pairs={{0,1},{1,2},{2,3},{4,5},{5,6},{6,7},{8,9},{9,10},{10,11},{12,13},{... | collective-permute-start | bytes 49160 | tf_op jit(solution)/shard_map/ppermute | solution.py:14
  175.1 9.8 %collective-permute-start.29 = (f32[2,4,512]{2,0,1:T(2,128)S(1)}, f32[2,4,512]{2,0,1:T(2,128)S(1)}, u32[]{:S(2)}, u32[]{:S(2)}) collective-permute-start(f32[2,4,512]{2,0,1:T(2,128)S(1)} %pad_maximum_fusion.46), channel_id=1, source_target_pairs={{1,0},{2,1},{3,2},{5,4},{6,5},{7,6},{9,8},{10,9},{11,10},{13,12},{... | collective-permute-start | bytes 49160 | tf_op jit(solution)/shard_map/ppermute | solution.py:14
  185.2 8.9 %collective-permute-start.30 = (f32[2,4,512]{2,0,1:T(2,128)S(1)}, f32[2,4,512]{2,0,1:T(2,128)S(1)}, u32[]{:S(2)}, u32[]{:S(2)}) collective-permute-start(f32[2,4,512]{2,0,1:T(2,128)S(1)} %pad_maximum_fusion.47), channel_id=1, source_target_pairs={{0,1},{1,2},{2,3},{4,5},{5,6},{6,7},{8,9},{9,10},{10,11},{12,13},{... | collective-permute-start | bytes 49160 | tf_op jit(solution)/shard_map/ppermute | solution.py:14
  307.0 10.1 %collective-permute-start.36 = (f32[2,16,512]{2,1,0:T(8,128)S(1)}, f32[2,16,512]{2,1,0:T(8,128)S(1)}, u32[]{:S(2)}, u32[]{:S(2)}) collective-permute-start(f32[2,16,512]{2,1,0:T(8,128)S(1)} %pad_maximum_fusion.18), channel_id=1, source_target_pairs={{4,0},{8,4},{12,8},{5,1},{9,5},{13,9},{6,2},{10,6},{14,10},{7,3},{... | collective-permute-start | bytes 196616 | tf_op jit(solution)/shard_map/ppermute | solution.py:14
  (64 other events, 315.1 us)
where the time goes:
time: 467 us; the launch traced here: 465 us
  starting transfers between devices  176 us (38%)
  blocking collectives  84.8 us (18%)
  local copies, waits for them, and re-layouts  81.9 us (18%)
  other arithmetic  66.8 us (14%)
  waiting for transfers between devices  44.9 us (10%)
  between operations  8.42 us (2%)
    ppermute x64, starting transfers between devices, from_behind(): lax.ppermute(value, axis, [(source, source + steps) for source in range(f...  176 us
    unnamed x1, blocking collectives  55.7 us
    gather x8, local copies, waits for them, and re-layouts, local(): records.append(electric[2].reshape(-1)[watched])  53.6 us
    scatter-add x8, other arithmetic, local(): driven = electric[2].reshape(-1).at[targets].add(amplitudes[step_index])....  49.1 us
    ppermute x64, waiting for transfers between devices, from_behind(): lax.ppermute(value, axis, [(source, source + steps) for source in range(f...  44.9 us
    all_gather x1, blocking collectives, local(): lax.all_gather(normalize(monitor_dft, own_weight), ('xy', 'gz'), axis=1,...  29 us
    unnamed x72, local copies, waits for them, and re-layouts  11 us
  transfers between devices with their start and end apart: 64, of which 27 were waited for; matrix products, arithmetic and copies ran while one was open for 14% of the time, Pallas kernels for 0%

commit v1 on v0

--- a/solution.py
+++ b/solution.py
@@ -6,6 +6,23 @@
 STEPS = 8
 NFREQ = 4
 STEP_RATIO = 0.5
+
+
+def in_order(blocks, dim):
+    blocks = jnp.moveaxis(blocks, 0, dim)
+    dims = blocks.shape
+    return blocks.reshape(*dims[:dim], dims[dim] * dims[dim + 1], *dims[dim + 2 :])
+
+
+def doubled(x, axis):
+    count, index = (lax.axis_size(axis), lax.axis_index(axis))
+    parts, stride = (x[None], 1)
+    while stride < count:
+        theirs = lax.ppermute(parts, axis, [(i, i ^ stride) for i in range(count)])
+        low = index & stride == 0
+        parts = jnp.concatenate([jnp.where(low, parts, theirs), jnp.where(low, theirs, parts)])
+        stride *= 2
+    return parts
 
 
 def from_behind(value, axis, steps):
@@ -137,9 +154,8 @@
     device_rank = lax.axis_index(("xy", "gz"))
     monitor_dft = lax.psum_scatter(bin_table, ("xy", "gz"), scatter_dimension=1, tiled=True)
     own_weight = lax.dynamic_slice_in_dim(bin_weight, device_rank * own_count, own_count)
-    coefficients = lax.all_gather(
-        normalize(monitor_dft, own_weight), ("xy", "gz"), axis=1, tiled=True
-    )
+    x = normalize(monitor_dft, own_weight)
+    coefficients = in_order(doubled(x, ("xy", "gz")), 1)
     picked = jnp.take(coefficients, source_bins.reshape(-1), axis=1)
     amplitudes = jnp.dot(source_kernel, picked, precision=lax.Precision.HIGHEST)
     targets = source_cells.reshape(-1)

time: 467 us -> 446 us (0.955)
  blocking collectives: 84.8 us -> 54.9 us
  starting transfers between devices: 176 us -> 186 us
    all_gather x1 -> x0, blocking collectives: 29 us -> none  [local(): lax.all_gather(normalize(monitor_dft, own_weight), ('xy', 'gz'), axis=1,...]
    ppermute x0 -> x4, starting transfers between devices: none -> 12.4 us  [doubled(): theirs = lax.ppermute(parts, axis, [(i, i ^ stride) for i in range(count)])]
    unnamed x72 -> x73, local copies, waits for them, and re-layouts: 11 us -> 10.2 us
  transfers between devices with their start and end apart: 64 -> 68, of which waited for: 27 -> 25; matrix products, arithmetic and copies ran while one was open for 14% -> 23% of each run, Pallas kernels for 0% -> 0%
where the time goes in v1:
time: 446 us; the launch traced here: 443 us
  starting transfers between devices  186 us (42%)
  local copies, waits for them, and re-layouts  79.9 us (18%)
  other arithmetic  65.8 us (15%)
  blocking collectives  54.9 us (12%)
  waiting for transfers between devices  46.4 us (10%)
  between operations  8.43 us (2%)
    ppermute x64, starting transfers between devices, from_behind(): lax.ppermute(value, axis, [(source, source + steps) for source in range(f...  174 us
    unnamed x1, blocking collectives  54.9 us
    gather x8, local copies, waits for them, and re-layouts, local(): records.append(electric[2].reshape(-1)[watched])  53.6 us
    scatter-add x8, other arithmetic, local(): driven = electric[2].reshape(-1).at[targets].add(amplitudes[step_index])....  49.3 us
    ppermute x64, waiting for transfers between devices, from_behind(): lax.ppermute(value, axis, [(source, source + steps) for source in range(f...  42.8 us
    ppermute x4, starting transfers between devices, doubled(): theirs = lax.ppermute(parts, axis, [(i, i ^ stride) for i in range(count)])  12.4 us
    unnamed x73, local copies, waits for them, and re-layouts  10.2 us
  transfers between devices with their start and end apart: 68, of which 25 were waited for; matrix products, arithmetic and copies ran while one was open for 23% of the time, Pallas kernels for 0%

profile of v1, /device:TPU:1, one launch (start us, length us, event | category | flops | bytes accessed | tf_op | source)
XLA Modules:
  0.0 443.4 jit_solution(13771406436302715497)
XLA Ops:
  26.6 5.2 %collective-permute-start.2 = (f32[2,4,512]{2,0,1:T(2,128)S(1)}, f32[2,4,512]{2,0,1:T(2,128)S(1)}, u32[]{:S(2)}, u32[]{:S(2)}) collective-permute-start(f32[2,4,512]{2,0,1:T(2,128)S(1)} %pad_maximum_fusion.34), channel_id=1, source_target_pairs={{0,1},{1,2},{2,3},{4,5},{5,6},{6,7},{8,9},{9,10},{10,11},{12,13},{... | collective-permute-start | bytes 49160 | tf_op jit(solution)/shard_map/ppermute | solution.py:31
  46.3 10.5 %gather_fusion = f32[1024]{0:T(1024)} fusion(f32[32768]{0:T(1024)S(1)} %bitcast.509, s32[1024]{0:T(1024)S(1)} %get-tuple-element.264), kind=kCustom, calls=%fused_computation | custom fusion | bytes 12288 | tf_op jit(solution)/shard_map/gather | solution.py:145
  70.9 6.2 %gather_fusion.1 = f32[1024]{0:T(1024)S(1)} fusion(f32[32768]{0:T(1024)S(1)} %bitcast.511, s32[1024]{0:T(1024)S(1)} %get-tuple-element.264), kind=kCustom, calls=%fused_computation.1 | custom fusion | bytes 12288 | tf_op jit(solution)/shard_map/gather | solution.py:145
  81.4 4.8 %collective-permute-start.11 = (f32[2,16,512]{2,1,0:T(8,128)S(1)}, f32[2,16,512]{2,1,0:T(8,128)S(1)}, u32[]{:S(2)}, u32[]{:S(2)}) collective-permute-start(f32[2,16,512]{2,1,0:T(8,128)S(1)} %pad_maximum_fusion.5), channel_id=1, source_target_pairs={{0,4},{4,8},{8,12},{1,5},{5,9},{9,13},{2,6},{6,10},{10,14},{3,7},{... | collective-permute-start | bytes 196616 | tf_op jit(solution)/shard_map/ppermute | solution.py:31
  91.3 6.2 %gather_fusion.2 = f32[1024]{0:T(1024)S(1)} fusion(f32[32768]{0:T(1024)S(1)} %bitcast.512, s32[1024]{0:T(1024)S(1)} %get-tuple-element.264), kind=kCustom, calls=%fused_computation.2 | custom fusion | bytes 12288 | tf_op jit(solution)/shard_map/gather | solution.py:145
  101.8 4.8 %collective-permute-start.15 = (f32[2,16,512]{2,1,0:T(8,128)S(1)}, f32[2,16,512]{2,1,0:T(8,128)S(1)}, u32[]{:S(2)}, u32[]{:S(2)}) collective-permute-start(f32[2,16,512]{2,1,0:T(8,128)S(1)} %pad_maximum_fusion.7), channel_id=1, source_target_pairs={{0,4},{4,8},{8,12},{1,5},{5,9},{9,13},{2,6},{6,10},{10,14},{3,7},{... | collective-permute-start | bytes 196616 | tf_op jit(solution)/shard_map/ppermute | solution.py:31
  111.6 6.2 %gather_fusion.3 = f32[1024]{0:T(1024)S(1)} fusion(f32[32768]{0:T(1024)S(1)} %bitcast.513, s32[1024]{0:T(1024)S(1)} %get-tuple-element.264), kind=kCustom, calls=%fused_computation.3 | custom fusion | bytes 12288 | tf_op jit(solution)/shard_map/gather | solution.py:145
  122.1 4.8 %collective-permute-start.19 = (f32[2,16,512]{2,1,0:T(8,128)S(1)}, f32[2,16,512]{2,1,0:T(8,128)S(1)}, u32[]{:S(2)}, u32[]{:S(2)}) collective-permute-start(f32[2,16,512]{2,1,0:T(8,128)S(1)} %pad_maximum_fusion.9), channel_id=1, source_target_pairs={{0,4},{4,8},{8,12},{1,5},{5,9},{9,13},{2,6},{6,10},{10,14},{3,7},{... | collective-permute-start | bytes 196616 | tf_op jit(solution)/shard_map/ppermute | solution.py:31
  131.9 6.2 %gather_fusion.4 = f32[1024]{0:T(1024)S(1)} fusion(f32[32768]{0:T(1024)S(1)} %bitcast.514, s32[1024]{0:T(1024)S(1)} %get-tuple-element.264), kind=kCustom, calls=%fused_computation.4 | custom fusion | bytes 12288 | tf_op jit(solution)/shard_map/gather | solution.py:145
  142.4 4.8 %collective-permute-start.23 = (f32[2,16,512]{2,1,0:T(8,128)S(1)}, f32[2,16,512]{2,1,0:T(8,128)S(1)}, u32[]{:S(2)}, u32[]{:S(2)}) collective-permute-start(f32[2,16,512]{2,1,0:T(8,128)S(1)} %pad_maximum_fusion.11), channel_id=1, source_target_pairs={{0,4},{4,8},{8,12},{1,5},{5,9},{9,13},{2,6},{6,10},{10,14},{3,7},{... | collective-permute-start | bytes 196616 | tf_op jit(solution)/shard_map/ppermute | solution.py:31
  152.2 6.2 %gather_fusion.5 = f32[1024]{0:T(1024)S(1)} fusion(f32[32768]{0:T(1024)S(1)} %bitcast.515, s32[1024]{0:T(1024)S(1)} %get-tuple-element.264), kind=kCustom, calls=%fused_computation.5 | custom fusion | bytes 12288 | tf_op jit(solution)/shard_map/gather | solution.py:145
  172.7 6.2 %gather_fusion.6 = f32[1024]{0:T(1024)S(1)} fusion(f32[32768]{0:T(1024)S(1)} %bitcast.516, s32[1024]{0:T(1024)S(1)} %get-tuple-element.264), kind=kCustom, calls=%fused_computation.6 | custom fusion | bytes 12288 | tf_op jit(solution)/shard_map/gather | solution.py:145
  189.7 6.2 %gather_fusion.7 = f32[1024]{0:T(1024)S(1)} fusion(f32[32768]{0:T(1024)S(1)} %bitcast.510, s32[1024]{0:T(1024)S(1)} %get-tuple-element.264), kind=kCustom, calls=%fused_computation.7 | custom fusion | bytes 12288 | tf_op jit(solution)/shard_map/gather | solution.py:145
  198.2 6.2 %scatter_custom_fusion = f32[128,8]{1,0:T(8,128)S(1)} fusion(s32[1024]{0:T(1024)} %bitcast.626, f32[1024,8]{1,0:T(8,128)S(1)} %fusion.306, f32[]{:T(128)} %constant.24.clone.1), kind=kCustom, calls=%fused_computation.498 | custom fusion | flops 8192 | bytes 4608 | tf_op jit(solution)/shard_map/scatter-add | solution.py:149
  204.4 54.9 %all-reduce.64 = f32[8,128]{0,1:T(8,128)S(1)} all-reduce(f32[8,128]{0,1:T(8,128)S(1)} %bitcast.606), channel_id=2, replica_groups=mesh['grp'=2,'xy'=4,'gz'=4] {'xy','gz'}, use_global_device_ids=true, to_apply=%region_1.2.clone | all-reduce | flops 1024 | bytes 8192
  263.1 4.9 %collective-permute-start.37 = (f32[2,8,8]{2,1,0:T(8,128)S(1)}, f32[2,8,8]{2,1,0:T(8,128)S(1)}, u32[]{:S(2)}, u32[]{:S(2)}) collective-permute-start(f32[2,8,8]{2,1,0:T(8,128)S(1)} %pad_maximum_fusion.66), channel_id=1, source_target_pairs={{0,2},{1,3},{2,0},{3,1},{4,6},{5,7},{6,4},{7,5},{8,10},{9,11},{10,... | collective-permute-start | bytes 1544 | tf_op jit(solution)/shard_map/ppermute | solution.py:21
  283.2 6.1 %scatter_fusion = f32[32768]{0:T(1024)S(1)} fusion(f32[32768]{0:T(1024)S(1)} %bitcast.501, s32[1024]{0:T(1024)S(1)} %bitcast.598, f32[1024]{0:T(1024)S(1)} %bitcast.614), kind=kCustom, calls=%fused_computation.10 | custom fusion | flops 1024 | bytes 16384 | tf_op jit(solution)/shard_map/scatter-add | solution.py:171
  304.8 6.1 %scatter_fusion.1 = f32[32768]{0:T(1024)S(1)} fusion(f32[32768]{0:T(1024)S(1)} %bitcast.502, s32[1024]{0:T(1024)S(1)} %bitcast.599, f32[1024]{0:T(1024)S(1)} %bitcast.613), kind=kCustom, calls=%fused_computation.11 | custom fusion | flops 1024 | bytes 16384 | tf_op jit(solution)/shard_map/scatter-add | solution.py:171
  326.9 6.4 %scatter_fusion.2 = f32[32768]{0:T(1024)S(1)} fusion(f32[32768]{0:T(1024)S(1)} %bitcast.503, s32[1024]{0:T(1024)S(1)} %bitcast.600, f32[1024]{0:T(1024)S(1)} %bitcast.612), kind=kCustom, calls=%fused_computation.12 | custom fusion | flops 1024 | bytes 16384 | tf_op jit(solution)/shard_map/scatter-add | solution.py:171
  349.2 6.1 %scatter_fusion.3 = f32[32768]{0:T(1024)S(1)} fusion(f32[32768]{0:T(1024)S(1)} %bitcast.504, s32[1024]{0:T(1024)S(1)} %bitcast.601, f32[1024]{0:T(1024)S(1)} %bitcast.611), kind=kCustom, calls=%fused_computation.13 | custom fusion | flops 1024 | bytes 16384 | tf_op jit(solution)/shard_map/scatter-add | solution.py:171
  371.3 6.1 %scatter_fusion.4 = f32[32768]{0:T(1024)S(1)} fusion(f32[32768]{0:T(1024)S(1)} %bitcast.505, s32[1024]{0:T(1024)S(1)} %bitcast.602, f32[1024]{0:T(1024)S(1)} %bitcast.610), kind=kCustom, calls=%fused_computation.14 | custom fusion | flops 1024 | bytes 16384 | tf_op jit(solution)/shard_map/scatter-add | solution.py:171
  393.4 6.1 %scatter_fusion.5 = f32[32768]{0:T(1024)S(1)} fusion(f32[32768]{0:T(1024)S(1)} %bitcast.506, s32[1024]{0:T(1024)S(1)} %bitcast.603, f32[1024]{0:T(1024)S(1)} %bitcast.609), kind=kCustom, calls=%fused_computation.15 | custom fusion | flops 1024 | bytes 16384 | tf_op jit(solution)/shard_map/scatter-add | solution.py:171
  415.5 6.1 %scatter_fusion.6 = f32[32768]{0:T(1024)S(1)} fusion(f32[32768]{0:T(1024)S(1)} %bitcast.507, s32[1024]{0:T(1024)S(1)} %bitcast.604, f32[1024]{0:T(1024)S(1)} %bitcast.608), kind=kCustom, calls=%fused_computation.16 | custom fusion | flops 1024 | bytes 16384 | tf_op jit(solution)/shard_map/scatter-add | solution.py:171
  436.1 6.1 %scatter_fusion.7 = f32[32768]{0:T(1024)S(1)} fusion(f32[32768]{0:T(1024)S(1)} %bitcast.508, s32[1024]{0:T(1024)S(1)} %bitcast.605, f32[1024]{0:T(1024)S(1)} %bitcast.607), kind=kCustom, calls=%fused_computation.17 | custom fusion | flops 1024 | bytes 16384 | tf_op jit(solution)/shard_map/scatter-add | solution.py:171
  (683 shorter events, 241.5 us)
Async XLA Ops:
  1.8 18.8 %collective-permute-start.1 = (f32[2,4,512]{2,0,1:T(2,128)S(1)}, f32[2,4,512]{2,0,1:T(2,128)S(1)}, u32[]{:S(2)}, u32[]{:S(2)}) collective-permute-start(f32[2,4,512]{2,0,1:T(2,128)S(1)} %pad_maximum_fusion.33), channel_id=1, source_target_pairs={{1,0},{2,1},{3,2},{5,4},{6,5},{7,6},{9,8},{10,9},{11,10},{13,12},{... | collective-permute-start | bytes 49160 | tf_op jit(solution)/shard_map/ppermute | solution.py:31
  3.3 17.4 %collective-permute-start = (f32[2,16,512]{2,1,0:T(8,128)S(1)}, f32[2,16,512]{2,1,0:T(8,128)S(1)}, u32[]{:S(2)}, u32[]{:S(2)}) collective-permute-start(f32[2,16,512]{2,1,0:T(8,128)S(1)} %pad_maximum_fusion), channel_id=1, source_target_pairs={{4,0},{8,4},{12,8},{5,1},{9,5},{13,9},{6,2},{10,6},{14,10},{7,3},{... | collective-permute-start | bytes 196616 | tf_op jit(solution)/shard_map/ppermute | solution.py:31
  6.4 14.3 %collective-permute-start.33 = (f32[2,4,512]{2,0,1:T(2,128)S(1)}, f32[2,4,512]{2,0,1:T(2,128)S(1)}, u32[]{:S(2)}, u32[]{:S(2)}) collective-permute-start(f32[2,4,512]{2,0,1:T(2,128)S(1)} %pad_maximum_fusion.49), channel_id=1, source_target_pairs={{1,0},{2,1},{3,2},{5,4},{6,5},{7,6},{9,8},{10,9},{11,10},{13,12},{... | collective-permute-start | bytes 49160 | tf_op jit(solution)/shard_map/ppermute | solution.py:31
  8.4 12.6 %collective-permute-start.32 = (f32[2,16,512]{2,1,0:T(8,128)}, f32[2,16,512]{2,1,0:T(8,128)}, u32[]{:S(2)}, u32[]{:S(2)}) collective-permute-start(f32[2,16,512]{2,1,0:T(8,128)} %pad_maximum_fusion.16), channel_id=1, source_target_pairs={{4,0},{8,4},{12,8},{5,1},{9,5},{13,9},{6,2},{10,6},{14,10},{7,3},{... | collective-permute-start | bytes 196616 | tf_op jit(solution)/shard_map/ppermute | solution.py:31
  22.0 18.5 %collective-permute-start.3 = (f32[2,16,512]{2,1,0:T(8,128)S(1)}, f32[2,16,512]{2,1,0:T(8,128)S(1)}, u32[]{:S(2)}, u32[]{:S(2)}) collective-permute-start(f32[2,16,512]{2,1,0:T(8,128)S(1)} %pad_maximum_fusion.1), channel_id=1, source_target_pairs={{0,4},{4,8},{8,12},{1,5},{5,9},{9,13},{2,6},{6,10},{10,14},{3,7},{... | collective-permute-start | bytes 196616 | tf_op jit(solution)/shard_map/ppermute | solution.py:31
  26.6 12.3 %collective-permute-start.2 = (f32[2,4,512]{2,0,1:T(2,128)S(1)}, f32[2,4,512]{2,0,1:T(2,128)S(1)}, u32[]{:S(2)}, u32[]{:S(2)}) collective-permute-start(f32[2,4,512]{2,0,1:T(2,128)S(1)} %pad_maximum_fusion.34), channel_id=1, source_target_pairs={{0,1},{1,2},{2,3},{4,5},{5,6},{6,7},{8,9},{9,10},{10,11},{12,13},{... | collective-permute-start | bytes 49160 | tf_op jit(solution)/shard_map/ppermute | solution.py:31
  40.8 16.1 %collective-permute-start.5 = (f32[2,4,512]{2,0,1:T(2,128)S(1)}, f32[2,4,512]{2,0,1:T(2,128)S(1)}, u32[]{:S(2)}, u32[]{:S(2)}) collective-permute-start(f32[2,4,512]{2,0,1:T(2,128)S(1)} %pad_maximum_fusion.35), channel_id=1, source_target_pairs={{1,0},{2,1},{3,2},{5,4},{6,5},{7,6},{9,8},{10,9},{11,10},{13,12},{... | collective-permute-start | bytes 49160 | tf_op jit(solution)/shard_map/ppermute | solution.py:31
  44.3 12.6 %collective-permute-start.4 = (f32[2,16,512]{2,1,0:T(8,128)S(1)}, f32[2,16,512]{2,1,0:T(8,128)S(1)}, u32[]{:S(2)}, u32[]{:S(2)}) collective-permute-start(f32[2,16,512]{2,1,0:T(8,128)S(1)} %pad_maximum_fusion.2), channel_id=1, source_target_pairs={{4,0},{8,4},{12,8},{5,1},{9,5},{13,9},{6,2},{10,6},{14,10},{7,3},{... | collective-permute-start | bytes 196616 | tf_op jit(solution)/shard_map/ppermute | solution.py:31
  67.5 9.6 %collective-permute-start.9 = (f32[2,4,512]{2,0,1:T(2,128)S(1)}, f32[2,4,512]{2,0,1:T(2,128)S(1)}, u32[]{:S(2)}, u32[]{:S(2)}) collective-permute-start(f32[2,4,512]{2,0,1:T(2,128)S(1)} %pad_maximum_fusion.37), channel_id=1, source_target_pairs={{1,0},{2,1},{3,2},{5,4},{6,5},{7,6},{9,8},{10,9},{11,10},{13,12},{... | collective-permute-start | bytes 49160 | tf_op jit(solution)/shard_map/ppermute | solution.py:31
  77.4 8.9 %collective-permute-start.10 = (f32[2,4,512]{2,0,1:T(2,128)S(1)}, f32[2,4,512]{2,0,1:T(2,128)S(1)}, u32[]{:S(2)}, u32[]{:S(2)}) collective-permute-start(f32[2,4,512]{2,0,1:T(2,128)S(1)} %pad_maximum_fusion.38), channel_id=1, source_target_pairs={{0,1},{1,2},{2,3},{4,5},{5,6},{6,7},{8,9},{9,10},{10,11},{12,13},{... | collective-permute-start | bytes 49160 | tf_op jit(solution)/shard_map/ppermute | solution.py:31
  87.8 9.6 %collective-permute-start.13 = (f32[2,4,512]{2,0,1:T(2,128)S(1)}, f32[2,4,512]{2,0,1:T(2,128)S(1)}, u32[]{:S(2)}, u32[]{:S(2)}) collective-permute-start(f32[2,4,512]{2,0,1:T(2,128)S(1)} %pad_maximum_fusion.39), channel_id=1, source_target_pairs={{1,0},{2,1},{3,2},{5,4},{6,5},{7,6},{9,8},{10,9},{11,10},{13,12},{... | collective-permute-start | bytes 49160 | tf_op jit(solution)/shard_map/ppermute | solution.py:31
  97.7 8.9 %collective-permute-start.14 = (f32[2,4,512]{2,0,1:T(2,128)S(1)}, f32[2,4,512]{2,0,1:T(2,128)S(1)}, u32[]{:S(2)}, u32[]{:S(2)}) collective-permute-start(f32[2,4,512]{2,0,1:T(2,128)S(1)} %pad_maximum_fusion.40), channel_id=1, source_target_pairs={{0,1},{1,2},{2,3},{4,5},{5,6},{6,7},{8,9},{9,10},{10,11},{12,13},{... | collective-permute-start | bytes 49160 | tf_op jit(solution)/shard_map/ppermute | solution.py:31
  108.1 9.6 %collective-permute-start.17 = (f32[2,4,512]{2,0,1:T(2,128)S(1)}, f32[2,4,512]{2,0,1:T(2,128)S(1)}, u32[]{:S(2)}, u32[]{:S(2)}) collective-permute-start(f32[2,4,512]{2,0,1:T(2,128)S(1)} %pad_maximum_fusion.41), channel_id=1, source_target_pairs={{1,0},{2,1},{3,2},{5,4},{6,5},{7,6},{9,8},{10,9},{11,10},{13,12},{... | collective-permute-start | bytes 49160 | tf_op jit(solution)/shard_map/ppermute | solution.py:31
  118.1 8.9 %collective-permute-start.18 = (f32[2,4,512]{2,0,1:T(2,128)S(1)}, f32[2,4,512]{2,0,1:T(2,128)S(1)}, u32[]{:S(2)}, u32[]{:S(2)}) collective-permute-start(f32[2,4,512]{2,0,1:T(2,128)S(1)} %pad_maximum_fusion.42), channel_id=1, source_target_pairs={{0,1},{1,2},{2,3},{4,5},{5,6},{6,7},{8,9},{9,10},{10,11},{12,13},{... | collective-permute-start | bytes 49160 | tf_op jit(solution)/shard_map/ppermute | solution.py:31
  128.5 9.6 %collective-permute-start.21 = (f32[2,4,512]{2,0,1:T(2,128)S(1)}, f32[2,4,512]{2,0,1:T(2,128)S(1)}, u32[]{:S(2)}, u32[]{:S(2)}) collective-permute-start(f32[2,4,512]{2,0,1:T(2,128)S(1)} %pad_maximum_fusion.43), channel_id=1, source_target_pairs={{1,0},{2,1},{3,2},{5,4},{6,5},{7,6},{9,8},{10,9},{11,10},{13,12},{... | collective-permute-start | bytes 49160 | tf_op jit(solution)/shard_map/ppermute | solution.py:31
  138.4 8.9 %collective-permute-start.22 = (f32[2,4,512]{2,0,1:T(2,128)S(1)}, f32[2,4,512]{2,0,1:T(2,128)S(1)}, u32[]{:S(2)}, u32[]{:S(2)}) collective-permute-start(f32[2,4,512]{2,0,1:T(2,128)S(1)} %pad_maximum_fusion.44), channel_id=1, source_target_pairs={{0,1},{1,2},{2,3},{4,5},{5,6},{6,7},{8,9},{9,10},{10,11},{12,13},{... | collective-permute-start | bytes 49160 | tf_op jit(solution)/shard_map/ppermute | solution.py:31
  148.8 9.6 %collective-permute-start.25 = (f32[2,4,512]{2,0,1:T(2,128)S(1)}, f32[2,4,512]{2,0,1:T(2,128)S(1)}, u32[]{:S(2)}, u32[]{:S(2)}) collective-permute-start(f32[2,4,512]{2,0,1:T(2,128)S(1)} %pad_maximum_fusion.45), channel_id=1, source_target_pairs={{1,0},{2,1},{3,2},{5,4},{6,5},{7,6},{9,8},{10,9},{11,10},{13,12},{... | collective-permute-start | bytes 49160 | tf_op jit(solution)/shard_map/ppermute | solution.py:31
  169.1 9.8 %collective-permute-start.29 = (f32[2,4,512]{2,0,1:T(2,128)S(1)}, f32[2,4,512]{2,0,1:T(2,128)S(1)}, u32[]{:S(2)}, u32[]{:S(2)}) collective-permute-start(f32[2,4,512]{2,0,1:T(2,128)S(1)} %pad_maximum_fusion.47), channel_id=1, source_target_pairs={{1,0},{2,1},{3,2},{5,4},{6,5},{7,6},{9,8},{10,9},{11,10},{13,12},{... | collective-permute-start | bytes 49160 | tf_op jit(solution)/shard_map/ppermute | solution.py:31
  303.5 9.7 %collective-permute-start.45 = (f32[2,4,512]{2,0,1:T(2,128)S(1)}, f32[2,4,512]{2,0,1:T(2,128)S(1)}, u32[]{:S(2)}, u32[]{:S(2)}) collective-permute-start(f32[2,4,512]{2,0,1:T(2,128)S(1)} %pad_maximum_fusion.54), channel_id=1, source_target_pairs={{1,0},{2,1},{3,2},{5,4},{6,5},{7,6},{9,8},{10,9},{11,10},{13,12},{... | collective-permute-start | bytes 49160 | tf_op jit(solution)/shard_map/ppermute | solution.py:31
  325.6 9.9 %collective-permute-start.49 = (f32[2,4,512]{2,0,1:T(2,128)S(1)}, f32[2,4,512]{2,0,1:T(2,128)S(1)}, u32[]{:S(2)}, u32[]{:S(2)}) collective-permute-start(f32[2,4,512]{2,0,1:T(2,128)S(1)} %pad_maximum_fusion.56), channel_id=1, source_target_pairs={{1,0},{2,1},{3,2},{5,4},{6,5},{7,6},{9,8},{10,9},{11,10},{13,12},{... | collective-permute-start | bytes 49160 | tf_op jit(solution)/shard_map/ppermute | solution.py:31
  347.9 9.7 %collective-permute-start.53 = (f32[2,4,512]{2,0,1:T(2,128)S(1)}, f32[2,4,512]{2,0,1:T(2,128)S(1)}, u32[]{:S(2)}, u32[]{:S(2)}) collective-permute-start(f32[2,4,512]{2,0,1:T(2,128)S(1)} %pad_maximum_fusion.58), channel_id=1, source_target_pairs={{1,0},{2,1},{3,2},{5,4},{6,5},{7,6},{9,8},{10,9},{11,10},{13,12},{... | collective-permute-start | bytes 49160 | tf_op jit(solution)/shard_map/ppermute | solution.py:31
  370.0 9.7 %collective-permute-start.57 = (f32[2,4,512]{2,0,1:T(2,128)S(1)}, f32[2,4,512]{2,0,1:T(2,128)S(1)}, u32[]{:S(2)}, u32[]{:S(2)}) collective-permute-start(f32[2,4,512]{2,0,1:T(2,128)S(1)} %pad_maximum_fusion.60), channel_id=1, source_target_pairs={{1,0},{2,1},{3,2},{5,4},{6,5},{7,6},{9,8},{10,9},{11,10},{13,12},{... | collective-permute-start | bytes 49160 | tf_op jit(solution)/shard_map/ppermute | solution.py:31
  392.0 9.7 %collective-permute-start.61 = (f32[2,4,512]{2,0,1:T(2,128)S(1)}, f32[2,4,512]{2,0,1:T(2,128)S(1)}, u32[]{:S(2)}, u32[]{:S(2)}) collective-permute-start(f32[2,4,512]{2,0,1:T(2,128)S(1)} %pad_maximum_fusion.62), channel_id=1, source_target_pairs={{1,0},{2,1},{3,2},{5,4},{6,5},{7,6},{9,8},{10,9},{11,10},{13,12},{... | collective-permute-start | bytes 49160 | tf_op jit(solution)/shard_map/ppermute | solution.py:31
  414.1 9.7 %collective-permute-start.65 = (f32[2,4,512]{2,0,1:T(2,128)S(1)}, f32[2,4,512]{2,0,1:T(2,128)S(1)}, u32[]{:S(2)}, u32[]{:S(2)}) collective-permute-start(f32[2,4,512]{2,0,1:T(2,128)S(1)} %pad_maximum_fusion.64), channel_id=1, source_target_pairs={{1,0},{2,1},{3,2},{5,4},{6,5},{7,6},{9,8},{10,9},{11,10},{13,12},{... | collective-permute-start | bytes 49160 | tf_op jit(solution)/shard_map/ppermute | solution.py:31
  (69 other events, 324.1 us)
